TPU v7x, 32 devices: a whole 2x2x4 slice. The times are simulated.
32 devices in a mesh: row: 8 (over z, core), col: 4 (over y, x).
Axes of the slice: x: 2, y: 2, z: 4, core: 2. Of those that a mesh axis runs over, the one named last changes fastest.
Arguments:
- example_grads: bfloat16 [1024, 4096], P(('row', 'col')), may hold values from -6 to 6
- val_grads: bfloat16 [64, 4096], P('row'), may hold values from -6 to 6
- val_weight: float32 [64], replicated, may hold values from 0.25 to 4
Outputs:
- gram: bfloat16 [1024, 640], P('row', 'col')
- weighted: float32 [1024, 64], P(('row', 'col'))
- scores: float32 [1024], P(('row', 'col'))
All inputs are finite; a program needn't handle non-finite values.
Results may differ from a plain program's by a relative error of at most 0.0034.
Values may be sent and summed in bfloat16 or wider, within the bound.
No kernel may reach another device: no remote copies, remote signals or barrier semaphores. Data moves between devices by JAX's collectives and lax.ppermute only.
A program may use at most 64 MiB of HBM per device.

v0:
```python
import jax
import jax.numpy as jnp
from jax import lax
from jax.sharding import PartitionSpec as P

step_size = 0.5


def on_device(example_grads, val_grads, val_weight):
    own_rows = example_grads.shape[0]
    feature_width = example_grads.shape[1]
    inverse = 1.0 / feature_width
    root_scale = feature_width ** (-0.5)
    row_count = lax.axis_size("row")
    half = row_count // 2
    slots = half + 1
    width = slots * own_rows
    row_place = lax.axis_index("row")
    offset = row_place * own_rows
    slot_of = jnp.tile(jnp.arange(slots * own_rows, dtype=jnp.int32) // own_rows, 1)
    dropped = jnp.logical_and(slot_of == half, row_place >= half)
    row_grads = lax.all_gather(example_grads, "col", axis=0, tiled=True)
    products = lax.dot_general(
        row_grads,
        lax.all_gather(example_grads, "row", axis=0, tiled=True),
        (((1,), (1,)), ((), ())),
        preferred_element_type=jnp.float32,
    )
    full_tile = (products * inverse).astype(jnp.bfloat16)
    packed = jnp.roll(full_tile, -offset, axis=1)[:, :width]
    gram_tile = jnp.where(dropped[None, :], jnp.zeros_like(packed), packed)
    all_val = lax.all_gather(val_grads, "row", axis=0, tiled=True)
    own_val = (
        lax.dot_general(
            example_grads, all_val, (((1,), (1,)), ((), ())), preferred_element_type=jnp.float32
        )
        * root_scale
    ).astype(jnp.bfloat16)
    column_val = lax.all_gather(own_val, "row", axis=0, tiled=True)
    partial_value = jnp.dot(full_tile, column_val, preferred_element_type=jnp.float32)
    weighted = lax.psum_scatter(partial_value, "col", scatter_dimension=0, tiled=True)
    val_count = val_weight.shape[0]
    scores = jnp.dot(
        own_val.astype(jnp.float32) - step_size * weighted,
        val_weight,
        precision=lax.Precision.HIGHEST,
    ) * val_count ** (-0.5)
    return (gram_tile, weighted, scores)


def solution(mesh):
    in_specs = (P(("row", "col"), None), P("row", None), P())
    out_specs = (P("row", "col"), P(("row", "col"), None), P(("row", "col")))
    return jax.shard_map(
        on_device, mesh=mesh, in_specs=in_specs, out_specs=out_specs, check_vma=False
    )
```

profile of v0, /device:TPU:0, one launch (start us, length us, event | category | flops | bytes accessed | tf_op | source)
XLA Modules:
  0.0 105.0 jit_solution(1984824861453080597)
XLA Ops:
  7.2 0.0 copy-start
  7.2 0.0 all-gather.3.cloned.1.call-start
  7.2 0.7 all-gather.3.cloned.1.call-update
  7.9 0.0 all-gather.5.cloned.1.call-start
  8.0 0.7 all-gather.5.cloned.1.call-update
  8.7 0.0 reduce-scatter.2.cloned.1.call-start
  8.7 16.7 %all_gather.14 = bf16[64,4096]{1,0:T(8,128)(2,1)S(1)} all-gather(bf16[8,4096]{1,0:T(8,128)(2,1)} %param.4), channel_id=1, replica_groups=mesh['row'=8,'col'=4] {'row'}, dimensions={0}, use_global_device_ids=true | all-gather | bytes 589824 | tf_op jit(solution)/shard_map/all_gather | solution.py:32
  25.4 1.2 %fusion.1 = bf16[32,64]{1,0:T(8,128)(2,1)S(1)} fusion(bf16[32,4096]{1,0:T(8,128)(2,1)} %param.3, bf16[64,4096]{1,0:T(8,128)(2,1)S(1)} %all_gather.14), kind=kOutput, calls=%fused_computation.3 | convolution fusion | flops 16781312 | bytes 790528 | tf_op jit(solution)/shard_map/dot_general | solution.py:34
  26.7 14.0 %all_gather.15 = bf16[256,64]{1,0:T(8,128)(2,1)S(1)} all-gather(bf16[32,64]{1,0:T(8,128)(2,1)S(1)} %fusion.1), channel_id=1, replica_groups=mesh['row'=8,'col'=4] {'row'}, dimensions={0}, use_global_device_ids=true | all-gather | bytes 36864 | tf_op jit(solution)/shard_map/all_gather | solution.py:39
  40.7 0.0 all-gather.3.cloned.1.call-done
  40.7 29.2 %all-gather.5.cloned.1.call-done = bf16[256,4096]{1,0:T(8,128)(2,1)} async-done(((bf16[32,4096]{1,0:T(8,128)(2,1)}), bf16[256,4096]{1,0:T(8,128)(2,1)}) %all-gather.5.cloned.1.call-update) | async-done | bytes 2097168 | tf_op jit(solution)/shard_map/all_gather | solution.py:25
  69.9 2.8 %fusion = bf16[128,256]{1,0:T(8,128)(2,1)S(1)} fusion(bf16[128,4096]{1,0:T(8,128)(2,1)} %all-gather.3.cloned.1.call-done, bf16[256,4096]{1,0:T(8,128)(2,1)} %all-gather.5.cloned.1.call-done), kind=kOutput, calls=%fused_computation.1 | convolution fusion | flops 268500992 | bytes 3211264 | tf_op jit(solution)/shard_map/dot_general | solution.py:23
  72.6 0.8 fusion.11
  73.4 0.0 reduce-scatter.2.cloned.1.call-update
  73.4 0.1 fusion.4
  73.6 0.7 copy.6
  74.3 22.8 %reduce-scatter.2.cloned.1.call-done = f32[32,64]{1,0:T(8,128)} async-done(((f32[128,64]{1,0:T(8,128)}), f32[32,64]{1,0:T(8,128)}) %reduce-scatter.2.cloned.1.call-update) | async-done | bytes 8208 | tf_op jit(solution)/shard_map/reduce_scatter | solution.py:41
  97.1 0.0 copy-done
  97.1 1.4 %fusion.2 = f32[32]{0:T(128)} fusion(f32[32,64]{1,0:T(8,128)} %reduce-scatter.2.cloned.1.call-done, bf16[32,64]{1,0:T(8,128)(2,1)S(1)} %fusion.1, f32[64]{0:T(128)S(1)} %copy-done), kind=kOutput, calls=%fused_computation.5 | convolution fusion | flops 30752 | bytes 12672 | tf_op jit(solution)/shard_map/dot_general | solution.py:43
  (1 shorter events, 0.0 us)
Async XLA Ops:
  7.2 89.9 %copy-start = (f32[64]{0:T(128)S(1)}, f32[64]{0:T(128)}, u32[]{:S(2)}) copy-start(f32[64]{0:T(128)} %param.5) | copy-start | bytes 772
  7.2 33.5 %all-gather.3.cloned.1.call-start = ((), (), s32[]{:S(2)}) async-start(), calls=%async_computation.1 | async-start | bytes 1310720 | tf_op jit(solution)/shard_map/all_gather | solution.py:22
  7.9 62.0 %all-gather.5.cloned.1.call-start = ((), (), s32[]{:S(2)}) async-start(), calls=%async_computation.2 | async-start | bytes 2359296 | tf_op jit(solution)/shard_map/all_gather | solution.py:25
  8.7 88.4 %reduce-scatter.2.cloned.1.call-start = ((), (), s32[]{:S(2)}) async-start(), calls=%async_computation.3 | async-start | bytes 81920 | tf_op jit(solution)/shard_map/reduce_scatter | solution.py:41
Sparse Core Ops, SparseCore 0:
  9.8 29.2 all-gather.2
  40.7 29.1 all-gather.4
  73.5 23.4 reduce-scatter.1
where the time goes:
time: 105 us
  waiting for transfers between devices  53.4 us (51%)
  blocking collectives  30.7 us (29%)
  between operations  13.8 us (13%)
  matrix products  6.11 us (6%)
    all_gather x1, waiting for transfers between devices, on_device(): lax.all_gather(example_grads, 'row', axis=0, tiled=True)  29.2 us
    reduce_scatter x1, waiting for transfers between devices, on_device(): lax.psum_scatter(partial_value, 'col', scatter_dimension=0, tiled=True)  22.8 us
    all_gather x1, blocking collectives, on_device(): all_val = lax.all_gather(val_grads, 'row', axis=0, tiled=True)  16.7 us
    all_gather x1, blocking collectives, on_device(): column_val = lax.all_gather(own_val, 'row', axis=0, tiled=True)  14 us
    dot_general x1, matrix products, on_device(): lax.dot_general(row_grads, lax.all_gather(example_grads, 'row', axis=0, t...  2.75 us
  transfers between devices with their start and end apart: 3, of which 2 were waited for; matrix products, arithmetic and copies ran while one was open for 2% of the time, Pallas kernels for 0%

commit v1 on v0

v1 whole, which is shorter than its diff:
```python
import jax
import jax.numpy as jnp
from jax import lax
from jax.experimental import pallas as pl
from jax.experimental.pallas import tpu as pltpu
from jax.sharding import PartitionSpec as P


step_size = 0.5


CONTRACT_LAST = (((1,), (1,)), ((), ()))
CONTRACT_FIRST = (((0,), (0,)), ((), ()))


def product(a, b, contract=CONTRACT_LAST):
    return lax.dot_general(a, b, contract, preferred_element_type=jnp.float32)


def place(col, k, count):
    return pl.ds(pl.multiple_of(jnp.bitwise_xor(col, k) * count, count), count)


def early_kernel(rows_total, cols_total, refs):
    half, quarter = rows_total // 2, rows_total // 4
    xy, same, other, vals_in = refs["xy"], refs["same"], refs["other"], refs["vals"]
    left, vals, row_val_ref = refs["left"], refs["all_vals"], refs["row_val"]
    right = refs["right"]
    count, width = xy[0].shape
    val_rows = vals_in[0].shape[0]
    row = lax.axis_index("row")
    col = lax.axis_index("col")
    low = lax.rem(row, 2) == 0
    for k in range(cols_total):
        left[place(col, k, count), :] = xy[k][...]
    for t in range(quarter):
        right[2 * t * count : (2 * t + 1) * count, :] = same[t][...]
    for t in range(quarter - 1):
        at = slice((2 * t + 1) * count, (2 * t + 2) * count)

        @pl.when(low)
        def _():
            right[at, :] = other[t][...]

        @pl.when(jnp.logical_not(low))
        def _():
            right[at, :] = other[t + 1][...]

    swapped = vals_in[half]
    for t in range(half):
        at = pl.multiple_of(lax.rem(row + 2 * t, rows_total) * val_rows, val_rows)
        vals[pl.ds(at, val_rows), :] = vals_in[t][...]
        near = jnp.bitwise_xor(row, 1)
        at = pl.multiple_of(lax.rem(near + 2 * t, rows_total) * val_rows, val_rows)
        vals[pl.ds(at, val_rows), :] = swapped[t * val_rows : (t + 1) * val_rows, :]
    root = width ** (-0.5)
    tile = (product(right[...], left[...]) * (1.0 / width)).astype(jnp.bfloat16)
    row_val = (product(left[...], vals[...]) * root).astype(jnp.bfloat16)
    col_val = (product(right[...], vals[...]) * root).astype(jnp.bfloat16)
    refs["tile"][...] = tile
    row_val_ref[...] = row_val
    refs["own_val"][...] = col_val[:count].astype(jnp.float32)
    refs["sums"][...] = product(tile, col_val, CONTRACT_FIRST)
    mirrored = jnp.dot(tile, row_val, preferred_element_type=jnp.float32)
    for j, ref in enumerate(refs["mirrored"], 1):
        ref[...] = mirrored[j * count : (j + 1) * count]


def late_kernel(rows_total, refs):
    half = rows_total // 2
    left, vals, row_val, right = refs["left"], refs["all_vals"], refs["row_val"], refs["right"]
    count, width = refs["same"].shape
    row = lax.axis_index("row")
    col = lax.axis_index("col")
    low = lax.rem(row, 2) == 0

    @pl.when(low)
    def _():
        right[:count, :] = refs["other_near"][...]

    @pl.when(jnp.logical_not(low))
    def _():
        right[:count, :] = refs["other_far"][...]

    right[count:, :] = refs["same"][...]
    tile = product(right[...], left[...]) * (1.0 / width)
    last = lax.broadcasted_iota(jnp.int32, tile.shape, 0) >= count
    dropped = jnp.logical_and(last, row >= half)
    tile = jnp.where(dropped, 0.0, tile).astype(jnp.bfloat16)
    col_val = (product(right[...], vals[...]) * width ** (-0.5)).astype(jnp.bfloat16)
    done = refs["tile"].shape[0]
    refs["gram"][:done, :] = refs["tile"][...]
    refs["gram"][done:, :] = tile
    refs["total"][...] = refs["sums"][...] + product(tile, col_val, CONTRACT_FIRST)
    mirrored = jnp.dot(tile, row_val[...], preferred_element_type=jnp.float32)
    for k, ref in enumerate(refs["direct"]):
        ref[...] = refs["total"][place(col, k, count), :]
    for j, ref in enumerate(refs["mirrored"]):
        ref[...] = mirrored[j * count : (j + 1) * count]


def call(body, ins, outs, scratch):
    groups = [(key, value) for part in (ins, outs, scratch) for key, value in part.items()]
    flat = lambda part: [v for value in part.values() for v in (value if isinstance(value, list) else [value])]

    def kernel(*refs):
        refs, named = list(refs), {}
        for key, value in groups:
            if isinstance(value, list):
                named[key], refs = refs[: len(value)], refs[len(value) :]
            else:
                named[key], refs = refs[0], refs[1:]
        body(named)

    vmem = pl.BlockSpec(memory_space=pltpu.VMEM)
    got = pl.pallas_call(
        kernel,
        out_shape=flat(outs),
        in_specs=[vmem] * len(flat(ins)),
        out_specs=[vmem] * len(flat(outs)),
        scratch_shapes=[pltpu.VMEM(s.shape, s.dtype) for s in flat(scratch)],
        compiler_params=pltpu.CompilerParams(vmem_limit_bytes=32 * 1024 * 1024),
    )(*flat(ins))
    got, named = list(got), {}
    for key, value in outs.items():
        if isinstance(value, list):
            named[key], got = got[: len(value)], got[len(value) :]
        else:
            named[key], got = got[0], got[1:]
    return named


def on_device(example_grads, val_grads, val_weight):
    count, width = example_grads.shape
    val_count = val_weight.shape[0]
    rows_total = lax.axis_size("row")
    cols_total = lax.axis_size("col")
    half, quarter = rows_total // 2, rows_total // 4
    slots, block = half + 1, cols_total * count
    assert rows_total % 4 == 0 and cols_total & (cols_total - 1) == 0

    def xor_col(value, k):
        return lax.ppermute(value, "col", [(i, i ^ k) for i in range(cols_total)])

    def from_row(value, j):
        return lax.ppermute(value, "row", [((i + j) % rows_total, i) for i in range(rows_total)])

    def swap(value):
        return lax.ppermute(value, "row", [(i ^ 1, i) for i in range(rows_total)])

    def to_row(value, j):
        senders = rows_total if j < half else half
        return lax.ppermute(value, "row", [(i, (i + j) % rows_total) for i in range(senders)])

    same = [example_grads]
    for _ in range(1, quarter):
        same.append(from_row(same[-1], 2))
    pairs = [((i + 2) % rows_total, i) for i in range(rows_total) if i % 2 == 0 or i < half]
    same.append(lax.ppermute(same[-1], "row", pairs))
    other = [swap(same[t]) for t in range(quarter + 1)]
    xy = [example_grads] + [xor_col(example_grads, k) for k in range(1, cols_total)]
    vals = [val_grads] + [from_row(val_grads, 2 * t) for t in range(1, half)]
    joined = jnp.concatenate(vals, axis=0)
    vals.append(swap(joined))

    f32 = lambda *shape: jax.ShapeDtypeStruct(shape, jnp.float32)
    bf16 = lambda *shape: jax.ShapeDtypeStruct(shape, jnp.bfloat16)
    early = call(
        lambda refs: early_kernel(rows_total, cols_total, refs),
        dict(xy=xy, same=same[:quarter], other=other[:quarter], vals=vals),
        dict(
            tile=bf16((slots - 2) * count, block),
            left=bf16(block, width),
            all_vals=bf16(val_count, width),
            row_val=bf16(block, val_count),
            own_val=f32(count, val_count),
            sums=f32(block, val_count),
            mirrored=[f32(count, val_count)] * (slots - 3),
        ),
        dict(right=bf16((slots - 2) * count, width)),
    )
    carried = {key: early[key] for key in ("tile", "left", "all_vals", "row_val", "sums")}
    late = call(
        lambda refs: late_kernel(rows_total, refs),
        dict(carried, same=same[quarter], other_near=other[quarter - 1], other_far=other[quarter]),
        dict(
            gram=bf16(slots * count, block),
            direct=[f32(count, val_count)] * cols_total,
            mirrored=[f32(count, val_count)] * 2,
        ),
        dict(right=bf16(2 * count, width), total=f32(block, val_count)),
    )
    mirrored = early["mirrored"] + late["mirrored"]
    weighted = late["direct"][0]
    for k in range(1, cols_total):
        weighted = weighted + xor_col(late["direct"][k], k)
    for j, value in enumerate(mirrored, 1):
        weighted = weighted + to_row(value, j)
    scaled = val_weight * val_count ** (-0.5)
    scores = jnp.sum((early["own_val"] - step_size * weighted) * scaled[None, :], axis=1)
    return late["gram"].T, weighted, scores


def solution(mesh):
    in_specs = (P(("row", "col"), None), P("row", None), P())
    out_specs = (P("row", "col"), P(("row", "col"), None), P(("row", "col")))

    return jax.shard_map(
        on_device, mesh=mesh, in_specs=in_specs, out_specs=out_specs, check_vma=False
    )
```

time: 105 us -> 44.7 us (0.43)
  waiting for transfers between devices: 53.4 us -> 12.3 us
  blocking collectives: 30.7 us -> 0 us
  starting transfers between devices: 0.11 us -> 26.8 us
  between operations: 13.8 us -> 0.79 us
  matrix products: 6.11 us -> 0 us
  Pallas kernels: 0 us -> 2.54 us
  other arithmetic: 0.14 us -> 2.1 us
    all_gather x2 -> x0, blocking collectives: 30.7 us -> none  [the longest x1 16.7 us: on_device(): all_val = lax.all_gather(val_grads, 'row', axis=0, tiled=True)]
    all_gather x2 -> x0, waiting for transfers between devices: 29.2 us -> none  [the longest x1 29.2 us: on_device(): lax.all_gather(example_grads, 'row', axis=0, tiled=True)]
    ppermute x0 -> x19, starting transfers between devices: none -> 26.8 us  [the longest x6 8.95 us: xor_col(): return lax.ppermute(value, 'col', [(i, i ^ k) for i in range(cols_total)])]
    reduce_scatter x1 -> x0, waiting for transfers between devices: 22.8 us -> none  [on_device(): lax.psum_scatter(partial_value, 'col', scatter_dimension=0, tiled=True)]
    ppermute x0 -> x19, waiting for transfers between devices: none -> 12.3 us  [the longest x4 6.25 us: from_row(): lax.ppermute(value, 'row', [((i + j) % rows_total, i) for i in range(rows...]
    dot_general x4 -> x0, matrix products: 6.11 us -> none  [the longest x1 2.75 us: on_device(): lax.dot_general(row_grads, lax.all_gather(example_grads, 'row', axis=0, t...]
    pallas_call x0 -> x2, Pallas kernels: none -> 2.54 us  [call(): pl.pallas_call(kernel, out_shape=flat(outs), in_specs=[vmem] * len(flat(i...]
    unnamed x3 -> x0, waiting for transfers between devices: 1.39 us -> none
  transfers between devices with their start and end apart: 3 -> 19, of which waited for: 2 -> 5; matrix products, arithmetic and copies ran while one was open for 2% -> 2% of each run, Pallas kernels for 0% -> 6%
where the time goes in v1:
time: 44.7 us; the launch traced here: 44.5 us
  starting transfers between devices  26.8 us (60%)
  waiting for transfers between devices  12.3 us (28%)
  Pallas kernels  2.54 us (6%)
  other arithmetic  2.1 us (5%)
  between operations  0.79 us (2%)
    ppermute x6, starting transfers between devices, xor_col(): return lax.ppermute(value, 'col', [(i, i ^ k) for i in range(cols_total)])  8.95 us
    ppermute x4, starting transfers between devices, from_row(): lax.ppermute(value, 'row', [((i + j) % rows_total, i) for i in range(rows...  7.16 us
    ppermute x4, waiting for transfers between devices, from_row(): lax.ppermute(value, 'row', [((i + j) % rows_total, i) for i in range(rows...  6.25 us
    ppermute x4, starting transfers between devices, to_row(): lax.ppermute(value, 'row', [(i, (i + j) % rows_total) for i in range(send...  5.61 us
    ppermute x1, starting transfers between devices, on_device(): same.append(lax.ppermute(same[-1], 'row', pairs))  5.03 us
    ppermute x1, waiting for transfers between devices, on_device(): same.append(lax.ppermute(same[-1], 'row', pairs))  3.95 us
    pallas_call x2, Pallas kernels, call(): pl.pallas_call(kernel, out_shape=flat(outs), in_specs=[vmem] * len(flat(i...  2.54 us
    ppermute x4, waiting for transfers between devices, to_row(): lax.ppermute(value, 'row', [(i, (i + j) % rows_total) for i in range(send...  1.37 us
  transfers between devices with their start and end apart: 19, of which 5 were waited for; matrix products, arithmetic and copies ran while one was open for 2% of the time, Pallas kernels for 6%

profile of v1, /device:TPU:0, one launch (start us, length us, event | category | flops | bytes accessed | tf_op | source)
XLA Modules:
  0.0 44.5 jit_solution(436357203745524589)
XLA Ops:
  0.6 5.1 %collective-permute-start.3 = (bf16[32,4096]{1,0:T(8,128)(2,1)}, bf16[32,4096]{1,0:T(8,128)(2,1)S(1)}, u32[]{:S(2)}, u32[]{:S(2)}) collective-permute-start(bf16[32,4096]{1,0:T(8,128)(2,1)} %refs_4_.1), channel_id=1, source_target_pairs={{8,0},{12,4},{16,8},{20,12},{24,16},{28,20},{0,24},{4,28},{9,1},{1... | collective-permute-start | bytes 786440 | tf_op jit(solution)/shard_map/ppermute | solution.py:146
  5.8 0.4 %collective-permute-start.6 = (bf16[8,4096]{1,0:T(8,128)(2,1)}, bf16[8,4096]{1,0:T(8,128)(2,1)S(1)}, u32[]{:S(2)}, u32[]{:S(2)}) collective-permute-start(bf16[8,4096]{1,0:T(8,128)(2,1)} %refs_8_.1), channel_id=1, source_target_pairs={{8,0},{12,4},{16,8},{20,12},{24,16},{28,20},{0,24},{4,28},{9,1},{1... | collective-permute-start | bytes 196616 | tf_op jit(solution)/shard_map/ppermute | solution.py:146
  6.2 1.6 %collective-permute-start.8 = (bf16[8,4096]{1,0:T(8,128)(2,1)}, bf16[8,4096]{1,0:T(8,128)(2,1)S(1)}, u32[]{:S(2)}, u32[]{:S(2)}) collective-permute-start(bf16[8,4096]{1,0:T(8,128)(2,1)} %refs_8_.1), channel_id=1, source_target_pairs={{24,0},{28,4},{0,8},{4,12},{8,16},{12,20},{16,24},{20,28},{25,1},{... | collective-permute-start | bytes 196616 | tf_op jit(solution)/shard_map/ppermute | solution.py:146
  7.8 1.5 %collective-permute-start = (bf16[32,4096]{1,0:T(8,128)(2,1)}, bf16[32,4096]{1,0:T(8,128)(2,1)S(1)}, u32[]{:S(2)}, u32[]{:S(2)}) collective-permute-start(bf16[32,4096]{1,0:T(8,128)(2,1)} %refs_4_.1), channel_id=1, source_target_pairs={{0,1},{1,0},{2,3},{3,2},{4,5},{5,4},{6,7},{7,6},{8,9},{9,8},{10,11... | collective-permute-start | bytes 786440 | tf_op jit(solution)/shard_map/ppermute | solution.py:143
  9.3 5.0 %collective-permute-done.6.refs_9_ = bf16[8,4096]{1,0:T(8,128)(2,1)S(1)} collective-permute-done((bf16[8,4096]{1,0:T(8,128)(2,1)}, bf16[8,4096]{1,0:T(8,128)(2,1)S(1)}, u32[]{:S(2)}, u32[]{:S(2)}) %collective-permute-start.6) | collective-permute-done | bytes 65568 | tf_op jit(solution)/shard_map/ppermute | solution.py:146
  14.3 1.5 %collective-permute-start.1 = (bf16[32,4096]{1,0:T(8,128)(2,1)}, bf16[32,4096]{1,0:T(8,128)(2,1)S(1)}, u32[]{:S(2)}, u32[]{:S(2)}) collective-permute-start(bf16[32,4096]{1,0:T(8,128)(2,1)} %refs_4_.1), channel_id=1, source_target_pairs={{0,2},{1,3},{2,0},{3,1},{4,6},{5,7},{6,4},{7,5},{8,10},{9,11},{10,... | collective-permute-start | bytes 786440 | tf_op jit(solution)/shard_map/ppermute | solution.py:143
  15.8 1.3 %collective-permute-done.7.refs_10_ = bf16[8,4096]{1,0:T(8,128)(2,1)S(1)} collective-permute-done((bf16[8,4096]{1,0:T(8,128)(2,1)}, bf16[8,4096]{1,0:T(8,128)(2,1)S(1)}, u32[]{:S(2)}, u32[]{:S(2)}) %collective-permute-start.7) | collective-permute-done | bytes 65568 | tf_op jit(solution)/shard_map/ppermute | solution.py:146
  17.1 2.4 %collective-permute-start.2 = (bf16[32,4096]{1,0:T(8,128)(2,1)}, bf16[32,4096]{1,0:T(8,128)(2,1)S(1)}, u32[]{:S(2)}, u32[]{:S(2)}) collective-permute-start(bf16[32,4096]{1,0:T(8,128)(2,1)} %refs_4_.1), channel_id=1, source_target_pairs={{0,3},{1,2},{2,1},{3,0},{4,7},{5,6},{6,5},{7,4},{8,11},{9,10},{10,... | collective-permute-start | bytes 786440 | tf_op jit(solution)/shard_map/ppermute | solution.py:143
  19.5 5.0 %collective-permute-start.10 = (bf16[32,4096]{1,0:T(8,128)(2,1)S(1)}, bf16[32,4096]{1,0:T(8,128)(2,1)S(1)}, u32[]{:S(2)}, u32[]{:S(2)}) collective-permute-start(bf16[32,4096]{1,0:T(8,128)(2,1)S(1)} %collective-permute-done.3.refs_5_), channel_id=1, source_target_pairs={{8,0},{12,4},{16,8},{20,12},{24,16},{0,24},{9,1},{13,5},{17,9},{21... | collective-permute-start | bytes 786440 | tf_op jit(solution)/shard_map/ppermute | solution.py:159
  24.6 0.9 %pad_maximum_fusion = bf16[32,4096]{1,0:T(8,128)(2,1)S(1)} fusion(bf16[8,4096]{1,0:T(8,128)(2,1)S(1)} %collective-permute-done.8.refs_11_, bf16[8,4096]{1,0:T(8,128)(2,1)S(1)} %collective-permute-done.7.refs_10_, bf16[8,4096]{1,0:T(8,128)(2,1)S(1)} %collective-permute-done.6.refs_9_, bf16[8,4096]{1,0:T(8,128)(2,1)} %refs_8_.1), kind=kLoop, calls=%fused_computation | loop fusion | flops 1048576 | bytes 524288 | tf_op jit(solution)/shard_map/concatenate | solution.py:163
  25.4 0.1 collective-permute-start.9
  25.5 0.7 %collective-permute-done.1.refs_2_ = bf16[32,4096]{1,0:T(8,128)(2,1)S(1)} collective-permute-done((bf16[32,4096]{1,0:T(8,128)(2,1)}, bf16[32,4096]{1,0:T(8,128)(2,1)S(1)}, u32[]{:S(2)}, u32[]{:S(2)}) %collective-permute-start.1) | collective-permute-done | bytes 262176 | tf_op jit(solution)/shard_map/ppermute | solution.py:143
  26.2 3.9 %collective-permute-done.10.refs_5_ = bf16[32,4096]{1,0:T(8,128)(2,1)S(1)} collective-permute-done((bf16[32,4096]{1,0:T(8,128)(2,1)S(1)}, bf16[32,4096]{1,0:T(8,128)(2,1)S(1)}, u32[]{:S(2)}, u32[]{:S(2)}) %collective-permute-start.10) | collective-permute-done | bytes 262176 | tf_op jit(solution)/shard_map/ppermute | solution.py:159
  30.2 1.2 %shard_map.58 = (bf16[96,128]{1,0:T(8,128)(2,1)S(1)}, bf16[128,4096]{1,0:T(8,128)(2,1)S(1)}, bf16[64,4096]{1,0:T(8,128)(2,1)S(1)}, bf16[128,64]{1,0:T(8,128)(2,1...) custom-call(bf16[32,4096]{1,0:T(8,128)(2,1)S(1)} %copy-done, ...), custom_call_target="tpu_custom_call" | custom-call | tf_op jit(solution)/shard_map/pallas_call | solution.py:116
  31.4 0.6 %collective-permute-start.15 = (f32[32,64]{1,0:T(8,128)S(1)}, f32[32,64]{1,0:T(8,128)S(1)}, u32[]{:S(2)}, u32[]{:S(2)}) collective-permute-start(f32[32,64]{1,0:T(8,128)S(1)} %get-tuple-element.28), channel_id=1, source_target_pairs={{0,4},{4,8},{8,12},{12,16},{16,20},{20,24},{24,28},{28,0},{1,5},{5... | collective-permute-start | bytes 24584 | tf_op jit(solution)/shard_map/ppermute | solution.py:153
  32.0 0.4 collective-permute-start.16
  32.4 1.3 %shard_map.59 = (bf16[160,128]{1,0:T(8,128)(2,1)}, f32[32,64]{1,0:T(8,128)S(1)}, f32[32,64]{1,0:T(8,128)S(1)}, f32[32,64]{1,0:T(8,128)S(1)}, f32[32,64]{1,0:T(8,...) custom-call(bf16[96,128]{1,0:T(8,128)(2,1)S(1)} %get-tuple-element.18.refs_0_, ...), custom_call_target="tpu_custom_call" | custom-call | tf_op jit(solution)/shard_map/pallas_call | solution.py:116
  33.7 0.5 %collective-permute-start.12 = (f32[32,64]{1,0:T(8,128)S(1)}, f32[32,64]{1,0:T(8,128)S(1)}, u32[]{:S(2)}, u32[]{:S(2)}) collective-permute-start(f32[32,64]{1,0:T(8,128)S(1)} %get-tuple-element.25), channel_id=1, source_target_pairs={{0,1},{1,0},{2,3},{3,2},{4,5},{5,4},{6,7},{7,6},{8,9},{9,8},{10,11... | collective-permute-start | bytes 24584 | tf_op jit(solution)/shard_map/ppermute | solution.py:143
  34.2 1.4 %collective-permute-start.13 = (f32[32,64]{1,0:T(8,128)S(1)}, f32[32,64]{1,0:T(8,128)S(1)}, u32[]{:S(2)}, u32[]{:S(2)}) collective-permute-start(f32[32,64]{1,0:T(8,128)S(1)} %get-tuple-element.26), channel_id=1, source_target_pairs={{0,2},{1,3},{2,0},{3,1},{4,6},{5,7},{6,4},{7,5},{8,10},{9,11},{10,... | collective-permute-start | bytes 24584 | tf_op jit(solution)/shard_map/ppermute | solution.py:143
  35.6 1.6 %collective-permute-start.14 = (f32[32,64]{1,0:T(8,128)S(1)}, f32[32,64]{1,0:T(8,128)S(1)}, u32[]{:S(2)}, u32[]{:S(2)}) collective-permute-start(f32[32,64]{1,0:T(8,128)S(1)} %get-tuple-element.27), channel_id=1, source_target_pairs={{0,3},{1,2},{2,1},{3,0},{4,7},{5,6},{6,5},{7,4},{8,11},{9,10},{10,... | collective-permute-start | bytes 24584 | tf_op jit(solution)/shard_map/ppermute | solution.py:143
  37.2 1.4 %collective-permute-start.17 = (f32[32,64]{1,0:T(8,128)S(1)}, f32[32,64]{1,0:T(8,128)S(1)}, u32[]{:S(2)}, u32[]{:S(2)}) collective-permute-start(f32[32,64]{1,0:T(8,128)S(1)} %get-tuple-element.30), channel_id=1, source_target_pairs={{0,12},{4,16},{8,20},{12,24},{16,28},{20,0},{24,4},{28,8},{1,13},{... | collective-permute-start | bytes 24584 | tf_op jit(solution)/shard_map/ppermute | solution.py:153
  38.6 3.3 %collective-permute-start.18 = (f32[32,64]{1,0:T(8,128)S(1)}, f32[32,64]{1,0:T(8,128)S(1)}, u32[]{:S(2)}, u32[]{:S(2)}) collective-permute-start(f32[32,64]{1,0:T(8,128)S(1)} %get-tuple-element.31), channel_id=1, source_target_pairs={{0,16},{4,20},{8,24},{12,28},{1,17},{5,21},{9,25},{13,29},{2,18},{... | collective-permute-start | bytes 24584 | tf_op jit(solution)/shard_map/ppermute | solution.py:153
  41.9 1.4 %collective-permute-done.18 = f32[32,64]{1,0:T(8,128)S(1)} collective-permute-done((f32[32,64]{1,0:T(8,128)S(1)}, f32[32,64]{1,0:T(8,128)S(1)}, u32[]{:S(2)}, u32[]{:S(2)}) %collective-permute-start.18) | collective-permute-done | bytes 8224 | tf_op jit(solution)/shard_map/ppermute | solution.py:153
  43.3 1.2 %multiply_reduce_fusion = (f32[32]{0:T(128)}, f32[32,64]{1,0:T(8,128)}) fusion(f32[32,64]{1,0:T(8,128)S(1)} %get-tuple-element.32, f32[64]{0:T(128)S(1)} %broadcast_multiply_fusion, f32[32,64]{1,0:T(8,128)S(1)} %collective-permute-done.18, f32[32,64]{1,0:T(8,128)S(1)} %collective-permute-done.17, f32[32,64]{1,0:T(8,128)S(1)} %collective-permute-done.16, ...), kind=kLoop, calls=%fused_computation.1 | loop fusion | flops 22496 | bytes 82304 | tf_op jit(solution)/shard_map/reduce_sum | solution.py:200
  (25 shorter events, 0.1 us)
Async XLA Ops:
  0.6 29.5 %copy-start = (bf16[32,4096]{1,0:T(8,128)(2,1)S(1)}, bf16[32,4096]{1,0:T(8,128)(2,1)}, u32[]{:S(2)}) copy-start(bf16[32,4096]{1,0:T(8,128)(2,1)} %refs_4_.1) | copy-start | bytes 786436
  0.6 29.5 %copy-start.1 = (bf16[8,4096]{1,0:T(8,128)(2,1)S(1)}, bf16[8,4096]{1,0:T(8,128)(2,1)}, u32[]{:S(2)}) copy-start(bf16[8,4096]{1,0:T(8,128)(2,1)} %refs_8_.1) | copy-start | bytes 196612
  0.6 18.9 %collective-permute-start.3 = (bf16[32,4096]{1,0:T(8,128)(2,1)}, bf16[32,4096]{1,0:T(8,128)(2,1)S(1)}, u32[]{:S(2)}, u32[]{:S(2)}) collective-permute-start(bf16[32,4096]{1,0:T(8,128)(2,1)} %refs_4_.1), channel_id=1, source_target_pairs={{8,0},{12,4},{16,8},{20,12},{24,16},{28,20},{0,24},{4,28},{9,1},{1... | collective-permute-start | bytes 786440 | tf_op jit(solution)/shard_map/ppermute | solution.py:146
  5.8 8.5 %collective-permute-start.6 = (bf16[8,4096]{1,0:T(8,128)(2,1)}, bf16[8,4096]{1,0:T(8,128)(2,1)S(1)}, u32[]{:S(2)}, u32[]{:S(2)}) collective-permute-start(bf16[8,4096]{1,0:T(8,128)(2,1)} %refs_8_.1), channel_id=1, source_target_pairs={{8,0},{12,4},{16,8},{20,12},{24,16},{28,20},{0,24},{4,28},{9,1},{1... | collective-permute-start | bytes 196616 | tf_op jit(solution)/shard_map/ppermute | solution.py:146
  6.2 10.8 %collective-permute-start.7 = (bf16[8,4096]{1,0:T(8,128)(2,1)}, bf16[8,4096]{1,0:T(8,128)(2,1)S(1)}, u32[]{:S(2)}, u32[]{:S(2)}) collective-permute-start(bf16[8,4096]{1,0:T(8,128)(2,1)} %refs_8_.1), channel_id=1, source_target_pairs={{16,0},{20,4},{24,8},{28,12},{0,16},{4,20},{8,24},{12,28},{17,1},{... | collective-permute-start | bytes 196616 | tf_op jit(solution)/shard_map/ppermute | solution.py:146
  6.2 13.3 %collective-permute-start.8 = (bf16[8,4096]{1,0:T(8,128)(2,1)}, bf16[8,4096]{1,0:T(8,128)(2,1)S(1)}, u32[]{:S(2)}, u32[]{:S(2)}) collective-permute-start(bf16[8,4096]{1,0:T(8,128)(2,1)} %refs_8_.1), channel_id=1, source_target_pairs={{24,0},{28,4},{0,8},{4,12},{8,16},{12,20},{16,24},{20,28},{25,1},{... | collective-permute-start | bytes 196616 | tf_op jit(solution)/shard_map/ppermute | solution.py:146
  7.8 17.6 %collective-permute-start = (bf16[32,4096]{1,0:T(8,128)(2,1)}, bf16[32,4096]{1,0:T(8,128)(2,1)S(1)}, u32[]{:S(2)}, u32[]{:S(2)}) collective-permute-start(bf16[32,4096]{1,0:T(8,128)(2,1)} %refs_4_.1), channel_id=1, source_target_pairs={{0,1},{1,0},{2,3},{3,2},{4,5},{5,4},{6,7},{7,6},{8,9},{9,8},{10,11... | collective-permute-start | bytes 786440 | tf_op jit(solution)/shard_map/ppermute | solution.py:143
  14.3 11.9 %collective-permute-start.1 = (bf16[32,4096]{1,0:T(8,128)(2,1)}, bf16[32,4096]{1,0:T(8,128)(2,1)S(1)}, u32[]{:S(2)}, u32[]{:S(2)}) collective-permute-start(bf16[32,4096]{1,0:T(8,128)(2,1)} %refs_4_.1), channel_id=1, source_target_pairs={{0,2},{1,3},{2,0},{3,1},{4,6},{5,7},{6,4},{7,5},{8,10},{9,11},{10,... | collective-permute-start | bytes 786440 | tf_op jit(solution)/shard_map/ppermute | solution.py:143
  17.1 13.1 %collective-permute-start.2 = (bf16[32,4096]{1,0:T(8,128)(2,1)}, bf16[32,4096]{1,0:T(8,128)(2,1)S(1)}, u32[]{:S(2)}, u32[]{:S(2)}) collective-permute-start(bf16[32,4096]{1,0:T(8,128)(2,1)} %refs_4_.1), channel_id=1, source_target_pairs={{0,3},{1,2},{2,1},{3,0},{4,7},{5,6},{6,5},{7,4},{8,11},{9,10},{10,... | collective-permute-start | bytes 786440 | tf_op jit(solution)/shard_map/ppermute | solution.py:143
  19.5 10.6 %collective-permute-start.4 = (bf16[32,4096]{1,0:T(8,128)(2,1)}, bf16[32,4096]{1,0:T(8,128)(2,1)S(1)}, u32[]{:S(2)}, u32[]{:S(2)}) collective-permute-start(bf16[32,4096]{1,0:T(8,128)(2,1)} %refs_4_.1), channel_id=1, source_target_pairs={{4,0},{0,4},{12,8},{8,12},{20,16},{16,20},{28,24},{24,28},{5,1},{1... | collective-permute-start | bytes 786440 | tf_op jit(solution)/shard_map/ppermute | solution.py:149
  19.5 10.6 %collective-permute-start.10 = (bf16[32,4096]{1,0:T(8,128)(2,1)S(1)}, bf16[32,4096]{1,0:T(8,128)(2,1)S(1)}, u32[]{:S(2)}, u32[]{:S(2)}) collective-permute-start(bf16[32,4096]{1,0:T(8,128)(2,1)S(1)} %collective-permute-done.3.refs_5_), channel_id=1, source_target_pairs={{8,0},{12,4},{16,8},{20,12},{24,16},{0,24},{9,1},{13,5},{17,9},{21... | collective-permute-start | bytes 786440 | tf_op jit(solution)/shard_map/ppermute | solution.py:159
  25.4 4.7 %collective-permute-start.9 = (bf16[32,4096]{1,0:T(8,128)(2,1)S(1)}, bf16[32,4096]{1,0:T(8,128)(2,1)S(1)}, u32[]{:S(2)}, u32[]{:S(2)}) collective-permute-start(bf16[32,4096]{1,0:T(8,128)(2,1)S(1)} %pad_maximum_fusion), channel_id=1, source_target_pairs={{4,0},{0,4},{12,8},{8,12},{20,16},{16,20},{28,24},{24,28},{5,1},{1... | collective-permute-start | bytes 786440 | tf_op jit(solution)/shard_map/ppermute | solution.py:149
  26.2 4.0 %collective-permute-start.5 = (bf16[32,4096]{1,0:T(8,128)(2,1)S(1)}, bf16[32,4096]{1,0:T(8,128)(2,1)S(1)}, u32[]{:S(2)}, u32[]{:S(2)}) collective-permute-start(bf16[32,4096]{1,0:T(8,128)(2,1)S(1)} %collective-permute-done.3.refs_5_), channel_id=1, source_target_pairs={{4,0},{0,4},{12,8},{8,12},{20,16},{16,20},{28,24},{24,28},{5,1},{1... | collective-permute-start | bytes 786440 | tf_op jit(solution)/shard_map/ppermute | solution.py:149
  30.1 2.2 %collective-permute-start.11 = (bf16[32,4096]{1,0:T(8,128)(2,1)S(1)}, bf16[32,4096]{1,0:T(8,128)(2,1)S(1)}, u32[]{:S(2)}, u32[]{:S(2)}) collective-permute-start(bf16[32,4096]{1,0:T(8,128)(2,1)S(1)} %collective-permute-done.10.refs_5_), channel_id=1, source_target_pairs={{4,0},{0,4},{12,8},{8,12},{20,16},{16,20},{28,24},{24,28},{5,1},{1... | collective-permute-start | bytes 786440 | tf_op jit(solution)/shard_map/ppermute | solution.py:149
  31.4 5.8 %collective-permute-start.15 = (f32[32,64]{1,0:T(8,128)S(1)}, f32[32,64]{1,0:T(8,128)S(1)}, u32[]{:S(2)}, u32[]{:S(2)}) collective-permute-start(f32[32,64]{1,0:T(8,128)S(1)} %get-tuple-element.28), channel_id=1, source_target_pairs={{0,4},{4,8},{8,12},{12,16},{16,20},{20,24},{24,28},{28,0},{1,5},{5... | collective-permute-start | bytes 24584 | tf_op jit(solution)/shard_map/ppermute | solution.py:153
  32.0 6.6 %collective-permute-start.16 = (f32[32,64]{1,0:T(8,128)S(1)}, f32[32,64]{1,0:T(8,128)S(1)}, u32[]{:S(2)}, u32[]{:S(2)}) collective-permute-start(f32[32,64]{1,0:T(8,128)S(1)} %get-tuple-element.29), channel_id=1, source_target_pairs={{0,8},{4,12},{8,16},{12,20},{16,24},{20,28},{24,0},{28,4},{1,9},{5... | collective-permute-start | bytes 24584 | tf_op jit(solution)/shard_map/ppermute | solution.py:153
  33.7 8.2 %collective-permute-start.12 = (f32[32,64]{1,0:T(8,128)S(1)}, f32[32,64]{1,0:T(8,128)S(1)}, u32[]{:S(2)}, u32[]{:S(2)}) collective-permute-start(f32[32,64]{1,0:T(8,128)S(1)} %get-tuple-element.25), channel_id=1, source_target_pairs={{0,1},{1,0},{2,3},{3,2},{4,5},{5,4},{6,7},{7,6},{8,9},{9,8},{10,11... | collective-permute-start | bytes 24584 | tf_op jit(solution)/shard_map/ppermute | solution.py:143
  34.2 7.7 %collective-permute-start.13 = (f32[32,64]{1,0:T(8,128)S(1)}, f32[32,64]{1,0:T(8,128)S(1)}, u32[]{:S(2)}, u32[]{:S(2)}) collective-permute-start(f32[32,64]{1,0:T(8,128)S(1)} %get-tuple-element.26), channel_id=1, source_target_pairs={{0,2},{1,3},{2,0},{3,1},{4,6},{5,7},{6,4},{7,5},{8,10},{9,11},{10,... | collective-permute-start | bytes 24584 | tf_op jit(solution)/shard_map/ppermute | solution.py:143
  35.6 6.3 %collective-permute-start.14 = (f32[32,64]{1,0:T(8,128)S(1)}, f32[32,64]{1,0:T(8,128)S(1)}, u32[]{:S(2)}, u32[]{:S(2)}) collective-permute-start(f32[32,64]{1,0:T(8,128)S(1)} %get-tuple-element.27), channel_id=1, source_target_pairs={{0,3},{1,2},{2,1},{3,0},{4,7},{5,6},{6,5},{7,4},{8,11},{9,10},{10,... | collective-permute-start | bytes 24584 | tf_op jit(solution)/shard_map/ppermute | solution.py:143
  37.2 4.7 %copy-start.2 = (f32[64]{0:T(128)S(1)}, f32[64]{0:T(128)}, u32[]{:S(2)}) copy-start(f32[64]{0:T(128)} %param.5) | copy-start | bytes 772
  37.2 4.7 %collective-permute-start.17 = (f32[32,64]{1,0:T(8,128)S(1)}, f32[32,64]{1,0:T(8,128)S(1)}, u32[]{:S(2)}, u32[]{:S(2)}) collective-permute-start(f32[32,64]{1,0:T(8,128)S(1)} %get-tuple-element.30), channel_id=1, source_target_pairs={{0,12},{4,16},{8,20},{12,24},{16,28},{20,0},{24,4},{28,8},{1,13},{... | collective-permute-start | bytes 24584 | tf_op jit(solution)/shard_map/ppermute | solution.py:153
  38.6 4.7 %collective-permute-start.18 = (f32[32,64]{1,0:T(8,128)S(1)}, f32[32,64]{1,0:T(8,128)S(1)}, u32[]{:S(2)}, u32[]{:S(2)}) collective-permute-start(f32[32,64]{1,0:T(8,128)S(1)} %get-tuple-element.31), channel_id=1, source_target_pairs={{0,16},{4,20},{8,24},{12,28},{1,17},{5,21},{9,25},{13,29},{2,18},{... | collective-permute-start | bytes 24584 | tf_op jit(solution)/shard_map/ppermute | solution.py:153
